TPU v7x, 32 devices: a whole 2x2x4 slice. The times are simulated.
32 devices in a mesh: view: 16 (over z, y, x), head: 2 (over core).
Axes of the slice: x: 2, y: 2, z: 4, core: 2. Of those that a mesh axis runs over, the one named last changes fastest.
Arguments:
- query_tokens: bfloat16 [4096, 1024], P('view'), may hold values from -360 to 360
- image_tokens: bfloat16 [16384, 1024], P('view'), may hold values from -6 to 6
- w_query: bfloat16 [1024, 1024], P(None, 'head'), may hold values from -0.1875 to 0.1875
- w_key: bfloat16 [1024, 1024], P(None, 'head'), may hold values from -0.1875 to 0.1875
- w_value: bfloat16 [1024, 1024], P(None, 'head'), may hold values from -0.1875 to 0.1875
- w_out: bfloat16 [1024, 1024], P('head'), may hold values from -0.1875 to 0.1875
- vis_list: int32 [32, 12], P('view'), may hold values from 0 to 127, as said below
- vis_count: int32 [32], P('view'), may hold values from 8 to 12
Outputs:
- attended: bfloat16 [4096, 1024], P('view', 'head')
Inputs may be any that keep to these rules, and one draw needn't show every extreme that they name: `vis_list`: entry j of row b names a global image block (block g holds image tokens g * 128 onward); the first vis_count[b] entries are the visible ones, the rest padding. All entries of one row lie on different devices of view. Among all entries of the 2 rows held by one device, those lying on one source device name the same block.
All inputs are finite; a program needn't handle non-finite values.
Results may differ from a plain program's by a relative error of at most 0.0085.
The roundings to bfloat16 on the way count: a program that leaves them out, or rounds other values in their place, can miss the bound.
Values may be sent and summed in bfloat16 or wider, within the bound.
A program may use at most 64 MiB of HBM per device.

v0:
```python
import math

import jax
import jax.numpy as jnp
from jax import lax
from jax.sharding import PartitionSpec as P

HEAD_DIM = 128
BLOCK = 128


def attend(query_heads, key_rows, visible, panel_width, head_count):
    groups, length = (key_rows.shape[0], key_rows.shape[1])
    key_heads = key_rows[:, :, :panel_width].reshape(groups, length, head_count, HEAD_DIM)
    value_heads = key_rows[:, :, panel_width:].reshape(groups, length, head_count, HEAD_DIM)
    scores = jnp.einsum(
        "qihd,qkhd->qhik", query_heads, key_heads, preferred_element_type=jnp.float32
    )
    scores = scores * (1.0 / math.sqrt(HEAD_DIM))
    allowed = visible[:, None, None, :]
    peak = jnp.max(jnp.where(allowed, scores, -1e30), axis=3, keepdims=True)
    raised = jnp.where(allowed, jnp.exp(scores - peak), 0.0)
    probs = (raised / jnp.sum(raised, axis=3, keepdims=True)).astype(jnp.bfloat16)
    context = jnp.einsum("qhik,qkhd->qihd", probs, value_heads, preferred_element_type=jnp.float32)
    return context.astype(jnp.bfloat16)


def per_device(query_tokens, image_tokens, w_query, w_key, w_value, w_out, vis_list, vis_count):
    view_count = lax.axis_size("view")
    panel_width = w_query.shape[1]
    head_count = panel_width // HEAD_DIM
    block_count = image_tokens.shape[0] // BLOCK
    query_blocks = vis_list.shape[0]
    queries = jnp.dot(query_tokens, w_query, preferred_element_type=jnp.float32).astype(
        jnp.bfloat16
    )
    image_keys = jnp.dot(image_tokens, w_key, preferred_element_type=jnp.float32).astype(
        jnp.bfloat16
    )
    image_values = jnp.dot(image_tokens, w_value, preferred_element_type=jnp.float32).astype(
        jnp.bfloat16
    )
    image_tiles = jnp.concatenate([image_keys, image_values], axis=1).reshape(
        block_count, BLOCK, 2 * panel_width
    )
    source = vis_list // block_count
    local_index = vis_list % block_count
    listed = jnp.arange(vis_list.shape[1], dtype=jnp.int32)[None, :] < vis_count[:, None]
    view_ids = jnp.arange(view_count, dtype=jnp.int32)
    matches = source[:, :, None] == view_ids[None, None, :]
    wanted = jnp.sum(jnp.where(matches, local_index[:, :, None], 0), axis=1)
    sourced = jnp.any(matches & listed[:, :, None], axis=1)
    asked_ids = lax.all_to_all(wanted, "view", split_axis=1, concat_axis=1, tiled=True)
    picked = jnp.take(image_tiles, asked_ids, axis=0)
    arrived = lax.all_to_all(picked, "view", split_axis=1, concat_axis=1, tiled=True)
    groups = arrived.shape[0]
    query_heads = queries.reshape(query_blocks, BLOCK, head_count, HEAD_DIM)
    key_rows = arrived.reshape(groups, -1, 2 * panel_width)
    visible = jnp.repeat(sourced, BLOCK, axis=1)
    context = attend(query_heads, key_rows, visible, panel_width, head_count)
    context = context.reshape(query_blocks * BLOCK, panel_width)
    partial_value = jnp.dot(context, w_out, preferred_element_type=jnp.float32)
    return lax.psum_scatter(partial_value, "head", scatter_dimension=1, tiled=True).astype(
        jnp.bfloat16
    )


def solution(mesh):
    return jax.shard_map(
        per_device,
        mesh=mesh,
        in_specs=(
            P("view", None),
            P("view", None),
            P(None, "head"),
            P(None, "head"),
            P(None, "head"),
            P("head", None),
            P("view", None),
            P("view"),
        ),
        out_specs=P("view", "head"),
        check_vma=False,
    )
```

profile of v0, /device:TPU:1, one launch (start us, length us, event | category | flops | bytes accessed | tf_op | source)
XLA Modules:
  0.0 302.8 jit_solution(4576486626460102009)
XLA Ops:
  6.5 0.8 and_select_fusion.1
  7.4 0.1 select_reduce_fusion.1
  7.5 0.7 copy.27
  8.2 7.4 %all-to-all-start = ((s32[2,16,1]{0,2,1:T(1,128)}), s32[2,16,1]{0,2,1:T(1,128)S(1)}, u32[]{:S(2)}, u32[]{:S(2)}) async-start(s32[2,16,1]{0,2,1:T(1,128)} %copy.27), calls=%async_computation | async-start | bytes 16384 | tf_op jit(solution)/shard_map/all_to_all | solution.py:53
  15.6 2.5 convolution_convert_fusion
  18.1 1.3 convolution_convert_fusion.1
  19.4 1.5 pad_maximum_fusion
  20.9 2.9 copy.38
  23.8 0.1 copy.30
  23.9 0.1 reshape.58
  24.0 0.1 copy.28
  24.1 0.1 copy.29
  24.2 4.8 %gather_fusion = bf16[32,128,1024]{2,1,0:T(8,128)(2,1)} fusion(bf16[8,128,1024]{2,1,0:T(8,128)(2,1)S(1)} %bitcast.34, s32[1024]{0:T(1024)S(1)} %pad_clamp_fusion), kind=kCustom, calls=%fused_computation | custom fusion | bytes 16777344 | tf_op jit(solution)/shard_map/jit(_take)/gather | solution.py:54
  29.0 7.5 %copy_select_fusion = bf16[2,16,128,1024]{3,2,0,1:T(8,128)(2,1)} fusion(bf16[2,16,128,1024]{3,2,1,0:T(8,128)(2,1)} %bitcast.35, pred[2,16]{0,1:T(8,128)(4,1)S(1)} %copy.29), kind=kLoop, calls=%fused_computation.2 | loop fusion | flops 4194304 | bytes 16777248 | tf_op jit(solution)/shard_map/jit(_take)/select_n | solution.py:54
  36.5 6.6 %all-to-all-start.1 = ((bf16[2,16,128,1024]{3,2,0,1:T(8,128)(2,1)}), bf16[2,16,128,1024]{3,2,0,1:T(8,128)(2,1)}, u32[]{:S(2)}, u32[]{:S(2)}) async-start(bf16[2,16,128,1024]{3,2,0,1:T(8,128)(2,1)} %copy_select_fusion), calls=%async_computation.1 | async-start | bytes 16777216 | tf_op jit(solution)/shard_map/all_to_all | solution.py:55
  43.1 0.2 reduce-scatter.2.cloned.1.call-start
  43.3 0.1 iota_compare_fusion.1
  43.4 0.1 fusion.24
  43.5 0.1 broadcast_bitcast_fusion
  43.6 0.4 convolution_convert_fusion.2
  44.0 0.1 reshape.53
  44.1 153.6 %all-to-all-done.1 = bf16[2,16,128,1024]{3,2,0,1:T(8,128)(2,1)} async-done(((bf16[2,16,128,1024]{3,2,0,1:T(8,128)(2,1)}), bf16[2,16,128,1024]{3,2,0,1:T(8,128)(2,1)}, u32[]{:S(2)}, u32[]{:S(2)}) %all-to-all-start.1) | async-done | bytes 8388640 | tf_op jit(solution)/shard_map/all_to_all | solution.py:55
  197.7 12.6 %copy.33 = bf16[2,16,128,1024]{2,1,3,0:T(8,128)(2,1)} copy(bf16[2,16,128,1024]{3,2,0,1:T(8,128)(2,1)} %all-to-all-done.1) | data formatting | bytes 16777216 | tf_op jit(solution)/shard_map/all_to_all | solution.py:55
  210.3 13.3 %reshape.51 = bf16[2,2048,1024]{1,2,0:T(8,128)(2,1)} reshape(bf16[2,16,128,1024]{2,1,3,0:T(8,128)(2,1)} %copy.33) | data formatting | bytes 16777216 | tf_op jit(solution)/shard_map/reshape | solution.py:58
  223.6 6.0 %fusion.27 = (bf16[2,2048,512]{1,2,0:T(8,128)(2,1)}, bf16[2,2048,512]{1,2,0:T(8,128)(2,1)}) fusion(bf16[2,2048,1024]{1,2,0:T(8,128)(2,1)} %reshape.51), kind=kLoop, calls=%fused_computation.44 | loop fusion | bytes 16777216 | tf_op jit(solution)/shard_map/slice | solution.py:14
  229.7 10.6 %fusion.28 = (f32[2,4,128]{2,1,0:T(4,128)S(1)}, f32[2,4,128,2048]{3,2,1,0:T(8,128)}) fusion(pred[2,2048]{1,0:T(4,128)(4,1)S(1)} %bitcast.39, bf16[2,2048,4,128]{1,3,2,0:T(8,128)(2,1)} %bitcast.37, bf16[2,128,4,128]{3,2,1,0:T(4,128)(2,1)S(1)} %reshape.53), kind=kOutput, calls=%fused_computation.45 | convolution fusion | flops 1086326784 | bytes 12853248 | tf_op jit(solution)/shard_map/sub | solution.py:22
  240.2 6.8 %fusion.10 = bf16[2,128,4,128]{1,3,2,0:T(8,128)(2,1)} fusion(bf16[2,2048,4,128]{1,3,2,0:T(8,128)(2,1)} %bitcast.36, f32[2,4,128,2048]{3,2,1,0:T(8,128)} %get-tuple-element.12, f32[2,4,128]{2,1,0:T(4,128)S(1)} %get-tuple-element.11), kind=kOutput, calls=%fused_computation.17 | convolution fusion | flops 541196288 | bytes 12849152 | tf_op jit(solution)/shard_map/qhik,qkhd->qihd/dot_general | solution.py:24
  247.1 1.1 copy.36
  248.2 1.4 fusion.13
  249.6 0.0 reduce-scatter.2.cloned.1.call-update
  249.6 44.5 %reduce-scatter.2.cloned.1.call-done = f32[256,512]{1,0:T(8,128)} async-done(((f32[256,1024]{1,0:T(8,128)}), f32[256,512]{1,0:T(8,128)}) %reduce-scatter.2.cloned.1.call-update) | async-done | bytes 524304 | tf_op jit(solution)/shard_map/reduce_scatter | solution.py:63
  294.1 1.8 convert_element_type.27
  (18 shorter events, 0.1 us)
Async XLA Ops:
  6.5 9.0 %copy-start = (bf16[1024,1024]{1,0:T(8,128)(2,1)S(1)}, bf16[1024,1024]{1,0:T(8,128)(2,1)}, u32[]{:S(2)}) copy-start(bf16[1024,1024]{1,0:T(8,128)(2,1)} %param.9) | copy-start | bytes 6291460
  6.5 11.6 %copy-start.5 = (bf16[1024,512]{1,0:T(8,128)(2,1)S(1)}, bf16[1024,512]{1,0:T(8,128)(2,1)}, u32[]{:S(2)}) copy-start(bf16[1024,512]{1,0:T(8,128)(2,1)} %param.11) | copy-start | bytes 3145732
  8.2 15.6 %all-to-all-start = ((s32[2,16,1]{0,2,1:T(1,128)}), s32[2,16,1]{0,2,1:T(1,128)S(1)}, u32[]{:S(2)}, u32[]{:S(2)}) async-start(s32[2,16,1]{0,2,1:T(1,128)} %copy.27), calls=%async_computation | async-start | bytes 16384 | tf_op jit(solution)/shard_map/all_to_all | solution.py:53
  36.5 6.8 %copy-start.6 = (s32[2]{0:T(128)S(1)}, s32[2]{0:T(128)}, u32[]{:S(2)}) copy-start(s32[2]{0:T(128)} %param.15) | copy-start | bytes 28
  36.5 7.1 %copy-start.2 = (bf16[1024,512]{1,0:T(8,128)(2,1)S(1)}, bf16[1024,512]{1,0:T(8,128)(2,1)}, u32[]{:S(2)}) copy-start(bf16[1024,512]{1,0:T(8,128)(2,1)} %param.10) | copy-start | bytes 3145732
  36.5 7.1 %copy-start.4 = (bf16[256,1024]{1,0:T(8,128)(2,1)S(1)}, bf16[256,1024]{1,0:T(8,128)(2,1)}, u32[]{:S(2)}) copy-start(bf16[256,1024]{1,0:T(8,128)(2,1)} %param.8) | copy-start | bytes 1572868
  36.5 161.2 %all-to-all-start.1 = ((bf16[2,16,128,1024]{3,2,0,1:T(8,128)(2,1)}), bf16[2,16,128,1024]{3,2,0,1:T(8,128)(2,1)}, u32[]{:S(2)}, u32[]{:S(2)}) async-start(bf16[2,16,128,1024]{3,2,0,1:T(8,128)(2,1)} %copy_select_fusion), calls=%async_computation.1 | async-start | bytes 16777216 | tf_op jit(solution)/shard_map/all_to_all | solution.py:55
  43.1 251.1 %reduce-scatter.2.cloned.1.call-start = ((), (), s32[]{:S(2)}) async-start(), calls=%async_computation.3 | async-start | bytes 1572864 | tf_op jit(solution)/shard_map/reduce_scatter | solution.py:63
  240.2 8.0 %copy-start.3 = (bf16[512,1024]{1,0:T(8,128)(2,1)S(1)}, bf16[512,1024]{1,0:T(8,128)(2,1)}, u32[]{:S(2)}) copy-start(bf16[512,1024]{1,0:T(8,128)(2,1)} %param.13) | copy-start | bytes 3145732
  240.2 55.7 %copy-start.1 = (bf16[1024,1024]{1,0:T(8,128)(2,1)S(1)}, bf16[1024,1024]{1,0:T(8,128)(2,1)}, u32[]{:S(2)}) copy-start(bf16[1024,1024]{1,0:T(8,128)(2,1)} %param.9) | copy-start | bytes 6291460
Sparse Core Ops, SparseCore 0:
  249.8 44.3 reduce-scatter.1
where the time goes:
time: 304 us; the launch traced here: 303 us
  waiting for transfers between devices  198 us (65%)
  local copies, waits for them, and re-layouts  41.9 us (14%)
  matrix products  23.1 us (8%)
  starting transfers between devices  14.2 us (5%)
  between operations  13.5 us (4%)
  other arithmetic  11.9 us (4%)
    all_to_all x1, waiting for transfers between devices, per_device(): lax.all_to_all(picked, 'view', split_axis=1, concat_axis=1, tiled=True)  154 us
    reduce_scatter x1, waiting for transfers between devices, per_device(): lax.psum_scatter(partial_value, 'head', scatter_dimension=1, tiled=True)  44.5 us
    reshape x1, local copies, waits for them, and re-layouts, per_device(): key_rows = arrived.reshape(groups, -1, 2 * panel_width)  13.3 us
    all_to_all x1, local copies, waits for them, and re-layouts, per_device(): lax.all_to_all(picked, 'view', split_axis=1, concat_axis=1, tiled=True)  12.6 us
    sub x1, matrix products, attend(): raised = jnp.where(allowed, jnp.exp(scores - peak), 0.0)  10.6 us
    select_n x1, other arithmetic, per_device(): picked = jnp.take(image_tiles, asked_ids, axis=0)  7.47 us
    all_to_all x1, starting transfers between devices, per_device(): lax.all_to_all(wanted, 'view', split_axis=1, concat_axis=1, tiled=True)  7.4 us
    dot_general x1, matrix products, attend(): jnp.einsum('qhik,qkhd->qihd', probs, value_heads, preferred_element_type=...  6.84 us
  transfers between devices with their start and end apart: 3, of which 2 were waited for; matrix products, arithmetic and copies ran while one was open for 3% of the time, Pallas kernels for 0%

commit v1 on v0

v1 whole, which is shorter than its diff:
```python
import functools
import math

import jax
import jax.numpy as jnp
from jax import lax
from jax.experimental import pallas as pl
from jax.experimental.pallas import tpu as pltpu
from jax.sharding import PartitionSpec as P

HEAD_DIM = 128
BLOCK = 128
GROUP = 4
MESH = pl.DeviceIdType.MESH
HIDDEN = -1e30


def offset_of(slot, view_count):
    return (view_count - slot) % view_count


def partner(index, offset, view_count):
    result, bit = 0, 1
    while bit < view_count:
        flip = (index // bit + offset // bit) % 2
        result = result + flip * bit
        bit *= 2
    return result


def kernel(
    n,
    heads,
    qt_hbm,
    x_hbm,
    wq_hbm,
    wk_hbm,
    wv_hbm,
    wo_hbm,
    own_ref,
    ask_ref,
    bias_ref,
    out_ref,
    x_vm,
    qt_vm,
    wq_vm,
    wk_vm,
    wv_vm,
    wo_all,
    asked_vm,
    asked_sm,
    picked,
    arrived,
    q_vm,
    k_vm,
    v_vm,
    peak_vm,
    total_vm,
    acc_vm,
    ctx_all,
    load_sem,
    ask_send,
    ask_recv,
    asked_sem,
    tok_send,
    tok_recv,
    fwd_send,
    fwd_recv,
    wo_send,
    wo_recv,
    ctx_send,
    ctx_recv,
):
    me = lax.axis_index("view")
    core = lax.axis_index("head")
    rows, width = out_ref.shape
    panel = wq_vm.shape[1]
    head_count = panel // HEAD_DIM
    depth = x_vm.shape[-1]
    groups = n // GROUP
    query_blocks = rows // BLOCK
    scale = 1.0 / math.sqrt(HEAD_DIM)

    def peer(slot):
        return (partner(me, offset_of(slot, n), n), core)

    def sibling(step):
        return (core + step) % heads

    def before(step):
        return (core + heads - step) % heads

    barrier = pltpu.get_barrier_semaphore()
    for slot in range(1, n):
        pl.semaphore_signal(barrier, inc=1, device_id=peer(slot), device_id_type=MESH)
    for step in range(1, heads):
        pl.semaphore_signal(
            barrier, inc=1, device_id=(me, sibling(step)), device_id_type=MESH
        )

    loads = [
        pltpu.make_async_copy(source, target, load_sem.at[position])
        for position, (source, target) in enumerate(
            [
                (x_hbm, x_vm),
                (qt_hbm, qt_vm),
                (wq_hbm, wq_vm),
                (wk_hbm, wk_vm),
                (wv_hbm, wv_vm),
                (
                    wo_hbm.at[:, pl.ds(pl.multiple_of(core * width, 128), width)],
                    wo_all.at[core],
                ),
            ]
        )
    ]
    for load in loads:
        load.start()
    pl.semaphore_wait(barrier, n - 1 + heads - 1)

    def ask(slot):
        return pltpu.make_async_remote_copy(
            src_ref=ask_ref.at[slot],
            dst_ref=asked_vm.at[slot],
            send_sem=ask_send.at[slot],
            recv_sem=ask_recv.at[slot],
            device_id=peer(slot),
            device_id_type=MESH,
        )

    def token(slot):
        return pltpu.make_async_remote_copy(
            src_ref=picked.at[slot],
            dst_ref=arrived.at[slot, core],
            send_sem=tok_send.at[slot],
            recv_sem=tok_recv.at[slot],
            device_id=peer(slot),
            device_id_type=MESH,
        )

    def forward(slot, step, part):
        return pltpu.make_async_remote_copy(
            src_ref=arrived.at[slot, part],
            dst_ref=arrived.at[slot, part],
            send_sem=fwd_send.at[slot, step],
            recv_sem=fwd_recv.at[slot, step],
            device_id=(me, sibling(step)),
            device_id_type=MESH,
        )

    def weight(step, part, columns):
        return pltpu.make_async_remote_copy(
            src_ref=wo_hbm.at[:, pl.ds(pl.multiple_of(columns * width, 128), width)],
            dst_ref=wo_all.at[part],
            send_sem=wo_send.at[step],
            recv_sem=wo_recv.at[step],
            device_id=(me, sibling(step)),
            device_id_type=MESH,
        )

    def context(step, head, part):
        lanes = pl.ds(head * HEAD_DIM, HEAD_DIM)
        return pltpu.make_async_remote_copy(
            src_ref=ctx_all.at[part, :, lanes],
            dst_ref=ctx_all.at[part, :, lanes],
            send_sem=ctx_send.at[step, head],
            recv_sem=ctx_recv.at[step, head],
            device_id=(me, sibling(step)),
            device_id_type=MESH,
        )

    for slot in range(1, n):
        ask(slot).start()
    for slot in range(1, n):
        ask(slot).wait_recv()
    rest = pl.ds(1, n - 1)
    fetch = pltpu.make_async_copy(asked_vm.at[rest], asked_sm.at[rest], asked_sem)
    fetch.start()
    loads[0].wait()
    fetch.wait()
    for slot in range(1, n):
        picked[slot] = x_vm[asked_sm[slot, 0, 0], core]
    for slot in range(1, n):
        token(slot).start()
    for step in range(1, heads):
        weight(step, core, sibling(step)).start()
    arrived[0] = x_vm[own_ref[0]]

    loads[1].wait()
    loads[2].wait()
    q_vm[...] = jnp.dot(
        qt_vm[...], wq_vm[...], preferred_element_type=jnp.float32
    ).astype(q_vm.dtype)
    peak_vm[...] = jnp.full_like(peak_vm, -3e38)
    total_vm[...] = jnp.zeros_like(total_vm)
    acc_vm[...] = jnp.zeros_like(acc_vm)
    loads[3].wait()
    loads[4].wait()

    def take_in(group):
        for member in range(GROUP):
            slot = group * GROUP + member

            @pl.when(slot > 0)
            def _():
                token(slot).wait_recv()
                for step in range(1, heads):
                    forward(slot, step, core).start()

    def settle(group):
        for member in range(GROUP):
            slot = group * GROUP + member

            @pl.when(slot > 0)
            def _():
                for step in range(1, heads):
                    forward(slot, step, before(step)).wait_recv()

    def attend(group):
        tokens = arrived[pl.ds(group * GROUP, GROUP)].reshape(GROUP * BLOCK, depth)
        k_vm[...] = jnp.dot(
            tokens, wk_vm[...], preferred_element_type=jnp.float32
        ).astype(k_vm.dtype)
        v_vm[...] = jnp.dot(
            tokens, wv_vm[...], preferred_element_type=jnp.float32
        ).astype(v_vm.dtype)
        bias = bias_ref[group]
        for head in range(head_count):
            lanes = pl.ds(head * HEAD_DIM, HEAD_DIM)
            scores = lax.dot_general(
                q_vm[:, lanes],
                k_vm[:, lanes],
                (((1,), (1,)), ((), ())),
                preferred_element_type=jnp.float32,
            )
            scores = scores * scale
            scores = (
                scores.reshape(query_blocks, BLOCK, GROUP * BLOCK) + bias
            ).reshape(rows, GROUP * BLOCK)
            old = peak_vm[head]
            new = jnp.maximum(old, jnp.max(scores, axis=1, keepdims=True))
            fade = jnp.exp(old - new)
            raised = jnp.exp(scores - new[:, :1])
            folded = raised[:, :BLOCK]
            for member in range(1, GROUP):
                folded = folded + raised[:, member * BLOCK : (member + 1) * BLOCK]
            peak_vm[head] = new
            total_vm[head] = total_vm[head] * fade + folded
            acc_vm[head] = acc_vm[head] * fade + jnp.dot(
                raised.astype(v_vm.dtype),
                v_vm[:, lanes],
                preferred_element_type=jnp.float32,
            )

    take_in(0)

    def advance(group, carry):
        @pl.when(group + 1 < groups)
        def _():
            take_in(group + 1)

        settle(group)
        attend(group)
        return carry

    lax.fori_loop(0, groups, advance, 0)

    for head in range(head_count):
        lanes = pl.ds(head * HEAD_DIM, HEAD_DIM)
        row_sum = jnp.sum(total_vm[head], axis=1, keepdims=True)
        ctx_all[core, :, lanes] = (acc_vm[head] / row_sum).astype(ctx_all.dtype)
        for step in range(1, heads):
            context(step, head, core).start()
    loads[5].wait()
    result = jnp.dot(
        ctx_all[core], wo_all[core], preferred_element_type=jnp.float32
    )
    for step in range(1, heads):
        part = before(step)
        weight(step, part, core).wait_recv()
        for head in range(head_count):
            context(step, head, part).wait_recv()
        result = result + jnp.dot(
            ctx_all[part], wo_all[part], preferred_element_type=jnp.float32
        )
    out_ref[...] = result.astype(out_ref.dtype)

    for slot in range(1, n):
        ask(slot).wait_send()
        token(slot).wait_send()
        for step in range(1, heads):
            forward(slot, step, core).wait_send()
    for step in range(1, heads):
        weight(step, core, sibling(step)).wait_send()
        for head in range(head_count):
            context(step, head, core).wait_send()


def per_device(query_tokens, image_tokens, w_query, w_key, w_value, w_out, vis_list, vis_count):
    n = lax.axis_size("view")
    heads = lax.axis_size("head")
    me = lax.axis_index("view")
    rows, depth = query_tokens.shape
    panel = w_query.shape[1]
    head_count = panel // HEAD_DIM
    width = w_out.shape[1] // heads
    block_count = image_tokens.shape[0] // BLOCK
    part_rows = BLOCK // heads
    query_blocks = vis_list.shape[0]
    groups = n // GROUP

    slots = jnp.arange(n, dtype=jnp.int32)
    sources = partner(me, offset_of(slots, n), n)
    matches = (vis_list // block_count)[:, :, None] == sources[None, None, :]
    listed = jnp.arange(vis_list.shape[1], dtype=jnp.int32)[None, :] < vis_count[:, None]
    sourced = jnp.any(matches & listed[:, :, None], axis=1)
    wanted = jnp.max(
        jnp.where(matches, (vis_list % block_count)[:, :, None], 0), axis=(0, 1)
    ).astype(jnp.int32)
    ask = jnp.broadcast_to(wanted[:, None, None], (n, 1, 128))
    bias = jnp.where(sourced, 0.0, HIDDEN).astype(jnp.float32)
    bias = jnp.repeat(bias, BLOCK, axis=1).reshape(query_blocks, groups, 1, GROUP * BLOCK)
    bias = jnp.transpose(bias, (1, 0, 2, 3))

    anywhere = pl.BlockSpec(memory_space=pl.ANY)
    vmem = pl.BlockSpec(memory_space=pltpu.VMEM)
    dtype = image_tokens.dtype
    dma = pltpu.SemaphoreType.DMA
    return pl.pallas_call(
        functools.partial(kernel, n, heads),
        out_shape=jax.ShapeDtypeStruct((rows, width), dtype),
        in_specs=[anywhere] * 6 + [pl.BlockSpec(memory_space=pltpu.SMEM), vmem, vmem],
        out_specs=vmem,
        scratch_shapes=[
            pltpu.VMEM((block_count, heads, part_rows, depth), dtype),
            pltpu.VMEM((rows, depth), dtype),
            pltpu.VMEM((depth, panel), dtype),
            pltpu.VMEM((depth, panel), dtype),
            pltpu.VMEM((depth, panel), dtype),
            pltpu.VMEM((heads, panel, width), dtype),
            pltpu.VMEM((n, 1, 128), jnp.int32),
            pltpu.SMEM((n, 1, 128), jnp.int32),
            pltpu.VMEM((n, part_rows, depth), dtype),
            pltpu.VMEM((n, heads, part_rows, depth), dtype),
            pltpu.VMEM((rows, panel), dtype),
            pltpu.VMEM((GROUP * BLOCK, panel), dtype),
            pltpu.VMEM((GROUP * BLOCK, panel), dtype),
            pltpu.VMEM((head_count, rows, HEAD_DIM), jnp.float32),
            pltpu.VMEM((head_count, rows, HEAD_DIM), jnp.float32),
            pltpu.VMEM((head_count, rows, HEAD_DIM), jnp.float32),
            pltpu.VMEM((heads, rows, panel), dtype),
            dma((6,)),
            dma((n,)),
            dma((n,)),
            dma,
            dma((n,)),
            dma((n,)),
            dma((n, heads)),
            dma((n, heads)),
            dma((heads,)),
            dma((heads,)),
            dma((heads, head_count)),
            dma((heads, head_count)),
        ],
        compiler_params=pltpu.CompilerParams(
            collective_id=0, has_side_effects=True, vmem_limit_bytes=52 * 2**20
        ),
    )(
        query_tokens,
        image_tokens.reshape(block_count, heads, part_rows, depth),
        w_query,
        w_key,
        w_value,
        w_out,
        wanted[:1],
        ask,
        bias,
    )


def solution(mesh):
    return jax.shard_map(
        per_device,
        mesh=mesh,
        in_specs=(
            P("view", None),
            P("view", None),
            P(None, "head"),
            P(None, "head"),
            P(None, "head"),
            P("head", None),
            P("view", None),
            P("view"),
        ),
        out_specs=P("view", "head"),
        check_vma=False,
    )
```

time: 304 us -> 78 us (0.26)
  waiting for transfers between devices: 198 us -> 0 us
  Pallas kernels: 0 us -> 73 us
  local copies, waits for them, and re-layouts: 41.9 us -> 3.15 us
  matrix products: 23.1 us -> 0 us
  starting transfers between devices: 14.2 us -> 0 us
  between operations: 13.5 us -> 0.03 us
  other arithmetic: 11.9 us -> 1.64 us
    all_to_all x2 -> x0, waiting for transfers between devices: 154 us -> none  [the longest x1 154 us: per_device(): lax.all_to_all(picked, 'view', split_axis=1, concat_axis=1, tiled=True)]
    pallas_call x0 -> x1, Pallas kernels: none -> 73 us  [per_device(): pl.pallas_call(functools.partial(kernel, n, heads), out_shape=jax.ShapeDt...]
    reduce_scatter x1 -> x0, waiting for transfers between devices: 44.5 us -> none  [per_device(): lax.psum_scatter(partial_value, 'head', scatter_dimension=1, tiled=True)]
    reshape x3 -> x0, local copies, waits for them, and re-layouts: 16.2 us -> none  [the longest x1 13.3 us: per_device(): key_rows = arrived.reshape(groups, -1, 2 * panel_width)]
    all_to_all x2 -> x0, starting transfers between devices: 14 us -> none  [the longest x1 7.4 us: per_device(): lax.all_to_all(wanted, 'view', split_axis=1, concat_axis=1, tiled=True)]
    all_to_all x2 -> x0, local copies, waits for them, and re-layouts: 13.3 us -> none  [the longest x1 12.6 us: per_device(): lax.all_to_all(picked, 'view', split_axis=1, concat_axis=1, tiled=True)]
    dot_general x5 -> x0, matrix products: 12.5 us -> none  [the longest x1 6.84 us: attend(): jnp.einsum('qhik,qkhd->qihd', probs, value_heads, preferred_element_type=...]
    sub x1 -> x0, matrix products: 10.6 us -> none  [attend(): raised = jnp.where(allowed, jnp.exp(scores - peak), 0.0)]
  transfers between devices with their start and end apart: 3 -> 0, of which waited for: 2 -> 0; matrix products, arithmetic and copies ran while one was open for 3% -> 0% of each run, Pallas kernels for 0% -> 0%
where the time goes in v1:
time: 78 us; the launch traced here: 77.8 us
  Pallas kernels  73 us (94%)
  local copies, waits for them, and re-layouts  3.15 us (4%)
  other arithmetic  1.64 us (2%)
    pallas_call x1, Pallas kernels, per_device(): pl.pallas_call(functools.partial(kernel, n, heads), out_shape=jax.ShapeDt...  73 us
    unnamed x5, local copies, waits for them, and re-layouts  2.97 us

profile of v1, /device:TPU:1, one launch (start us, length us, event | category | flops | bytes accessed | tf_op | source)
XLA Modules:
  0.0 77.8 jit_solution(12516811053153154731)
XLA Ops:
  0.0 0.7 iota_compare_fusion
  0.8 0.7 and_select_fusion.9
  1.4 0.1 fusion
  1.5 0.1 fusion.1
  1.6 0.1 broadcast_in_dim.37.ask_ref
  1.7 0.1 broadcast_in_dim.40
  1.8 0.0 copy-start
  1.9 1.2 %copy-done = bf16[1024,512]{1,0:T(8,128)(2,1)S(1)} copy-done((bf16[1024,512]{1,0:T(8,128)(2,1)S(1)}, bf16[1024,512]{1,0:T(8,128)(2,1)}, u32[]{:S(2)}) %copy-start) | copy-done | bytes 1048600
  3.1 0.0 copy-start.1
  3.1 1.0 %copy-done.1 = bf16[256,1024]{1,0:T(8,128)(2,1)S(1)} copy-done((bf16[256,1024]{1,0:T(8,128)(2,1)S(1)}, bf16[256,1024]{1,0:T(8,128)(2,1)}, u32[]{:S(2)}) %copy-start.1) | copy-done | bytes 524312
  4.1 73.0 %shard_map.82 = bf16[256,512]{1,0:T(8,128)(2,1)S(1)} custom-call(bf16[256,1024]{1,0:T(8,128)(2,1)S(1)} %copy-done.1, bf16[8,2,64,1024]{3,2,1,0:T(8,128)(2,1)} %bitcast.7, bf16[1024,512]{1,0:T(8,128)(2,1)S(1)} %copy-done, bf16[1024,512]{1,0:T(8,128)(2,1)} %wk_hbm.1, bf16[1024,512]{1,0:T(8,128)(2,1)} %wv_hbm.1, bf16[512,1024]{1,0:T(8,128)(2,1)} %wo_hbm.1, ...), custom_call_target="tpu_custom_call" | custom-call | tf_op jit(solution)/shard_map/pallas_call | solution.py:329
  77.1 0.7 copy.16
  (4 shorter events, 0.1 us)
Async XLA Ops:
  1.8 1.2 %copy-start = (bf16[1024,512]{1,0:T(8,128)(2,1)S(1)}, bf16[1024,512]{1,0:T(8,128)(2,1)}, u32[]{:S(2)}) copy-start(bf16[1024,512]{1,0:T(8,128)(2,1)} %wq_hbm.1) | copy-start | bytes 3145732
  3.1 1.0 %copy-start.1 = (bf16[256,1024]{1,0:T(8,128)(2,1)S(1)}, bf16[256,1024]{1,0:T(8,128)(2,1)}, u32[]{:S(2)}) copy-start(bf16[256,1024]{1,0:T(8,128)(2,1)} %qt_hbm.1) | copy-start | bytes 1572868

commit v2 on v1

--- a/solution.py
+++ b/solution.py
@@ -16,10 +16,11 @@
 
 
 def offset_of(slot, view_count):
-    return (view_count - slot) % view_count
-
-
-def partner(index, offset, view_count):
+    half = view_count // 2
+    return slot % half + half * (1 - slot // half)
+
+
+def flipped(index, offset, view_count):
     result, bit = 0, 1
     while bit < view_count:
         flip = (index // bit + offset // bit) % 2
@@ -58,6 +59,11 @@
     total_vm,
     acc_vm,
     ctx_all,
+    bias_in,
+    part_out,
+    part_in,
+    stat_out,
+    stat_in,
     load_sem,
     ask_send,
     ask_recv,
@@ -70,6 +76,8 @@
     wo_recv,
     ctx_send,
     ctx_recv,
+    mate_send,
+    mate_recv,
 ):
     me = lax.axis_index("view")
     core = lax.axis_index("head")
@@ -77,12 +85,18 @@
     panel = wq_vm.shape[1]
     head_count = panel // HEAD_DIM
     depth = x_vm.shape[-1]
-    groups = n // GROUP
+    half = n // 2
+    set_groups = half // GROUP
     query_blocks = rows // BLOCK
     scale = 1.0 / math.sqrt(HEAD_DIM)
 
     def peer(slot):
-        return (partner(me, offset_of(slot, n), n), core)
+        return (flipped(me, offset_of(slot, n), n), core)
+
+    def holder(slot):
+        return (flipped(me, slot % half, n), core)
+
+    mate = (flipped(me, half, n), core)
 
     def sibling(step):
         return (core + step) % heads
@@ -91,7 +105,9 @@
         return (core + heads - step) % heads
 
     barrier = pltpu.get_barrier_semaphore()
-    for slot in range(1, n):
+    asked_slots = [slot for slot in range(n) if slot != half]
+    sent_slots = [slot for slot in range(n) if slot % half]
+    for slot in asked_slots:
         pl.semaphore_signal(barrier, inc=1, device_id=peer(slot), device_id_type=MESH)
     for step in range(1, heads):
         pl.semaphore_signal(
@@ -116,7 +132,7 @@
     ]
     for load in loads:
         load.start()
-    pl.semaphore_wait(barrier, n - 1 + heads - 1)
+    pl.semaphore_wait(barrier, len(asked_slots) + heads - 1)
 
     def ask(slot):
         return pltpu.make_async_remote_copy(
@@ -134,7 +150,7 @@
             dst_ref=arrived.at[slot, core],
             send_sem=tok_send.at[slot],
             recv_sem=tok_recv.at[slot],
-            device_id=peer(slot),
+            device_id=holder(slot),
             device_id_type=MESH,
         )
 
@@ -169,31 +185,56 @@
             device_id_type=MESH,
         )
 
-    for slot in range(1, n):
+    def to_mate(position, source, target):
+        return pltpu.make_async_remote_copy(
+            src_ref=source,
+            dst_ref=target,
+            send_sem=mate_send.at[position],
+            recv_sem=mate_recv.at[position],
+            device_id=mate,
+            device_id_type=MESH,
+        )
+
+    def partial(head):
+        lanes = pl.ds(head * HEAD_DIM, HEAD_DIM)
+        return to_mate(3 + head, part_out.at[:, lanes], part_in.at[:, lanes])
+
+    lend = to_mate(0, q_vm.at[1], q_vm.at[0])
+    hint = to_mate(1, bias_ref.at[pl.ds(0, set_groups)], bias_in)
+    stats = to_mate(2, stat_out, stat_in)
+
+    for slot in asked_slots:
         ask(slot).start()
-    for slot in range(1, n):
+    hint.start()
+    loads[1].wait()
+    loads[2].wait()
+    q_vm[1] = jnp.dot(
+        qt_vm[...], wq_vm[...], preferred_element_type=jnp.float32
+    ).astype(q_vm.dtype)
+    lend.start()
+    loads[0].wait()
+    for slot in asked_slots:
         ask(slot).wait_recv()
-    rest = pl.ds(1, n - 1)
-    fetch = pltpu.make_async_copy(asked_vm.at[rest], asked_sm.at[rest], asked_sem)
-    fetch.start()
-    loads[0].wait()
-    fetch.wait()
-    for slot in range(1, n):
+    fetches = [
+        pltpu.make_async_copy(
+            asked_vm.at[pl.ds(start, size)],
+            asked_sm.at[pl.ds(start, size)],
+            asked_sem.at[position],
+        )
+        for position, (start, size) in enumerate([(0, half), (half + 1, half - 1)])
+    ]
+    for fetch in fetches:
+        fetch.start()
+    for fetch in fetches:
+        fetch.wait()
+    for slot in sent_slots:
         picked[slot] = x_vm[asked_sm[slot, 0, 0], core]
-    for slot in range(1, n):
+    for slot in sent_slots:
         token(slot).start()
     for step in range(1, heads):
         weight(step, core, sibling(step)).start()
-    arrived[0] = x_vm[own_ref[0]]
-
-    loads[1].wait()
-    loads[2].wait()
-    q_vm[...] = jnp.dot(
-        qt_vm[...], wq_vm[...], preferred_element_type=jnp.float32
-    ).astype(q_vm.dtype)
-    peak_vm[...] = jnp.full_like(peak_vm, -3e38)
-    total_vm[...] = jnp.zeros_like(total_vm)
-    acc_vm[...] = jnp.zeros_like(acc_vm)
+    arrived[0] = x_vm[asked_sm[0, 0, 0]]
+    arrived[half] = x_vm[own_ref[0]]
     loads[3].wait()
     loads[4].wait()
 
@@ -201,7 +242,7 @@
         for member in range(GROUP):
             slot = group * GROUP + member
 
-            @pl.when(slot > 0)
+            @pl.when(slot % half > 0)
             def _():
                 token(slot).wait_recv()
                 for step in range(1, heads):
@@ -211,12 +252,12 @@
         for member in range(GROUP):
             slot = group * GROUP + member
 
-            @pl.when(slot > 0)
+            @pl.when(slot % half > 0)
             def _():
                 for step in range(1, heads):
                     forward(slot, step, before(step)).wait_recv()
 
-    def attend(group):
+    def attend(group, own, bias):
         tokens = arrived[pl.ds(group * GROUP, GROUP)].reshape(GROUP * BLOCK, depth)
         k_vm[...] = jnp.dot(
             tokens, wk_vm[...], preferred_element_type=jnp.float32
@@ -224,11 +265,10 @@
         v_vm[...] = jnp.dot(
             tokens, wv_vm[...], preferred_element_type=jnp.float32
         ).astype(v_vm.dtype)
-        bias = bias_ref[group]
         for head in range(head_count):
             lanes = pl.ds(head * HEAD_DIM, HEAD_DIM)
             scores = lax.dot_general(
-                q_vm[:, lanes],
+                q_vm[own, :, lanes],
                 k_vm[:, lanes],
                 (((1,), (1,)), ((), ())),
                 preferred_element_type=jnp.float32,
@@ -252,23 +292,58 @@
                 preferred_element_type=jnp.float32,
             )
 
-    take_in(0)
-
-    def advance(group, carry):
-        @pl.when(group + 1 < groups)
-        def _():
-            take_in(group + 1)
-
-        settle(group)
-        attend(group)
-        return carry
-
-    lax.fori_loop(0, groups, advance, 0)
-
+    def reset():
+        peak_vm[...] = jnp.full_like(peak_vm, -3e38)
+        total_vm[...] = jnp.zeros_like(total_vm)
+        acc_vm[...] = jnp.zeros_like(acc_vm)
+
+    def row_sums(head):
+        folded = jnp.sum(total_vm[head], axis=1, keepdims=True)
+        return jnp.broadcast_to(folded, (rows, HEAD_DIM))
+
+    def attend_set(own):
+        first = own * set_groups
+        last = first + set_groups
+        reset()
+        take_in(first)
+
+        def advance(group, carry):
+            @pl.when(group + 1 < last)
+            def _():
+                take_in(group + 1)
+
+            settle(group)
+            attend(group, own, bias_ref[group] if own else bias_in[group])
+            return carry
+
+        lax.fori_loop(first, last, advance, 0)
+
+    lend.wait_recv()
+    hint.wait_recv()
+    attend_set(0)
     for head in range(head_count):
         lanes = pl.ds(head * HEAD_DIM, HEAD_DIM)
-        row_sum = jnp.sum(total_vm[head], axis=1, keepdims=True)
-        ctx_all[core, :, lanes] = (acc_vm[head] / row_sum).astype(ctx_all.dtype)
+        part_out[:, lanes] = acc_vm[head].astype(part_out.dtype)
+        partial(head).start()
+        stat_out[pl.ds(2 * head, 1), :] = peak_vm[head].T[:1]
+        stat_out[pl.ds(2 * head + 1, 1), :] = row_sums(head).T[:1]
+    stats.start()
+    attend_set(1)
+    stats.wait_recv()
+    for head in range(head_count):
+        lanes = pl.ds(head * HEAD_DIM, HEAD_DIM)
+        partial(head).wait_recv()
+
+        def spread(row):
+            return jnp.broadcast_to(stat_in[pl.ds(row, 1), :], (HEAD_DIM, rows)).T
+
+        peak, mate_peak = peak_vm[head], spread(2 * head)
+        top = jnp.maximum(peak, mate_peak)
+        weight_own = jnp.exp(peak - top)
+        weight_mate = jnp.exp(mate_peak - top)
+        row_sum = row_sums(head) * weight_own + spread(2 * head + 1) * weight_mate
+        merged = acc_vm[head] * weight_own + part_in[:, lanes] * weight_mate
+        ctx_all[core, :, lanes] = (merged / row_sum).astype(ctx_all.dtype)
         for step in range(1, heads):
             context(step, head, core).start()
     loads[5].wait()
@@ -285,11 +360,14 @@
         )
     out_ref[...] = result.astype(out_ref.dtype)
 
-    for slot in range(1, n):
+    for slot in asked_slots:
         ask(slot).wait_send()
+    for slot in sent_slots:
         token(slot).wait_send()
         for step in range(1, heads):
             forward(slot, step, core).wait_send()
+    for copy in [lend, hint, stats] + [partial(head) for head in range(head_count)]:
+        copy.wait_send()
     for step in range(1, heads):
         weight(step, core, sibling(step)).wait_send()
         for head in range(head_count):
@@ -310,7 +388,7 @@
     groups = n // GROUP
 
     slots = jnp.arange(n, dtype=jnp.int32)
-    sources = partner(me, offset_of(slots, n), n)
+    sources = flipped(me, offset_of(slots, n), n)
     matches = (vis_list // block_count)[:, :, None] == sources[None, None, :]
     listed = jnp.arange(vis_list.shape[1], dtype=jnp.int32)[None, :] < vis_count[:, None]
     sourced = jnp.any(matches & listed[:, :, None], axis=1)
@@ -342,17 +420,22 @@
             pltpu.SMEM((n, 1, 128), jnp.int32),
             pltpu.VMEM((n, part_rows, depth), dtype),
             pltpu.VMEM((n, heads, part_rows, depth), dtype),
-            pltpu.VMEM((rows, panel), dtype),
+            pltpu.VMEM((2, rows, panel), dtype),
             pltpu.VMEM((GROUP * BLOCK, panel), dtype),
             pltpu.VMEM((GROUP * BLOCK, panel), dtype),
             pltpu.VMEM((head_count, rows, HEAD_DIM), jnp.float32),
             pltpu.VMEM((head_count, rows, HEAD_DIM), jnp.float32),
             pltpu.VMEM((head_count, rows, HEAD_DIM), jnp.float32),
             pltpu.VMEM((heads, rows, panel), dtype),
+            pltpu.VMEM((groups // 2,) + bias.shape[1:], jnp.float32),
+            pltpu.VMEM((rows, panel), dtype),
+            pltpu.VMEM((rows, panel), dtype),
+            pltpu.VMEM((2 * head_count, rows), jnp.float32),
+            pltpu.VMEM((2 * head_count, rows), jnp.float32),
             dma((6,)),
             dma((n,)),
             dma((n,)),
-            dma,
+            dma((2,)),
             dma((n,)),
             dma((n,)),
             dma((n, heads)),
@@ -361,9 +444,11 @@
             dma((heads,)),
             dma((heads, head_count)),
             dma((heads, head_count)),
+            dma((3 + head_count,)),
+            dma((3 + head_count,)),
         ],
         compiler_params=pltpu.CompilerParams(
-            collective_id=0, has_side_effects=True, vmem_limit_bytes=52 * 2**20
+            collective_id=0, has_side_effects=True, vmem_limit_bytes=60 * 2**20
         ),
     )(
         query_tokens,
@@ -372,7 +457,7 @@
         w_key,
         w_value,
         w_out,
-        wanted[:1],
+        wanted[n // 2 : n // 2 + 1],
         ask,
         bias,
     )

time: 78 us -> 60.4 us (0.77)
  the two profiles are of different devices: /device:TPU:1 before, /device:TPU:25 now
where the time goes in v2:
time: 60.4 us; the launch traced here: 60 us
  Pallas kernels  54.7 us (91%)
  local copies, waits for them, and re-layouts  3.66 us (6%)
  other arithmetic  1.64 us (3%)
    pallas_call x1, Pallas kernels, per_device(): pl.pallas_call(functools.partial(kernel, n, heads), out_shape=jax.ShapeDt...  54.7 us
    unnamed x1, local copies, waits for them, and re-layouts  1.67 us

profile of v2, /device:TPU:25, one launch (start us, length us, event | category | flops | bytes accessed | tf_op | source)
XLA Modules:
  0.0 60.0 jit_solution(17828032199365917692)
XLA Ops:
  0.0 0.7 %iota_compare_fusion = pred[2,12]{1,0:T(4,128)(4,1)S(1)} fusion(s32[2]{0:T(128)} %param.15), kind=kLoop, calls=%fused_computation.27 | loop fusion | flops 24 | bytes 32 | tf_op jit(solution)/shard_map/lt | solution.py:393
  0.8 0.7 %and_select_fusion.10 = (s32[2,12]{1,0:T(2,128)S(1)}, s32[2,12]{1,0:T(2,128)S(1)}) fusion(s32[2,12]{1,0:T(2,128)} %param.14), kind=kLoop, calls=%fused_computation.23 | loop fusion | flops 456 | bytes 288 | tf_op jit(solution)/shard_map/jit(floor_divide)/jit(_where)/select_n | solution.py:392
  1.4 0.1 fusion
  1.5 0.6 %slice.3.own_ref = s32[1]{0:T(128)} slice(s32[16]{0:T(128)S(1)} %fusion), slice={[8:9]} | slice | bytes 8 | tf_op jit(solution)/shard_map/slice | solution.py:460
  2.1 0.1 fusion.1
  2.2 0.7 %broadcast_in_dim.37.ask_ref = s32[16,1,128]{2,1,0:T(1,128)} broadcast(s32[16]{0:T(128)S(1)} %fusion), dimensions={0} | broadcast | bytes 8256 | tf_op jit(solution)/shard_map/broadcast_in_dim | solution.py:398
  2.9 0.1 broadcast_in_dim.40
  3.0 0.6 %copy.14 = f32[2,4,1,512]{3,2,0,1:T(1,128)} copy(f32[2,4,1,512]{3,1,0,2:T(4,128)S(1)} %reshape_reshape.3) | data formatting | bytes 32768 | tf_op jit(solution)/shard_map/reshape;reshape | solution.py:400
  3.6 54.7 %shard_map.82 = bf16[256,512]{1,0:T(8,128)(2,1)} custom-call(bf16[256,1024]{1,0:T(8,128)(2,1)} %qt_hbm.1, bf16[8,2,64,1024]{3,2,1,0:T(8,128)(2,1)} %bitcast.4, bf16[1024,512]{1,0:T(8,128)(2,1)} %wq_hbm.1, bf16[1024,512]{1,0:T(8,128)(2,1)} %wk_hbm.1, bf16[1024,512]{1,0:T(8,128)(2,1)} %wv_hbm.1, bf16[512,1024]{1,0:T(8,128)(2,1)} %wo_hbm.1, s32[1]{0:T(128)} %slice.3.own_ref, ...), custom_call_target="tpu_custom_call" | custom-call | tf_op jit(solution)/shard_map/pallas_call | solution.py:407
  58.4 1.7 %copy.16 = bf16[256,512]{1,0:T(8,128)(2,1)} copy(bf16[256,512]{1,0:T(8,128)(2,1)} %shard_map.82) | data formatting | bytes 524288
  (3 shorter events, 0.0 us)

commit v3 on v2

--- a/solution.py
+++ b/solution.py
@@ -10,7 +10,7 @@
 
 HEAD_DIM = 128
 BLOCK = 128
-GROUP = 4
+GROUP = 2
 MESH = pl.DeviceIdType.MESH
 HIDDEN = -1e30
 
@@ -130,8 +130,13 @@
             ]
         )
     ]
-    for load in loads:
-        load.start()
+    for position in (1, 2, 0, 3, 4, 5):
+        loads[position].start()
+    loads[1].wait()
+    loads[2].wait()
+    q_vm[1] = jnp.dot(
+        qt_vm[...], wq_vm[...], preferred_element_type=jnp.float32
+    ).astype(q_vm.dtype)
     pl.semaphore_wait(barrier, len(asked_slots) + heads - 1)
 
     def ask(slot):
@@ -205,13 +210,8 @@
 
     for slot in asked_slots:
         ask(slot).start()
+    lend.start()
     hint.start()
-    loads[1].wait()
-    loads[2].wait()
-    q_vm[1] = jnp.dot(
-        qt_vm[...], wq_vm[...], preferred_element_type=jnp.float32
-    ).astype(q_vm.dtype)
-    lend.start()
     loads[0].wait()
     for slot in asked_slots:
         ask(slot).wait_recv()
@@ -400,7 +400,7 @@
     bias = jnp.repeat(bias, BLOCK, axis=1).reshape(query_blocks, groups, 1, GROUP * BLOCK)
     bias = jnp.transpose(bias, (1, 0, 2, 3))
 
-    anywhere = pl.BlockSpec(memory_space=pl.ANY)
+    anywhere = pl.BlockSpec(memory_space=pltpu.HBM)
     vmem = pl.BlockSpec(memory_space=pltpu.VMEM)
     dtype = image_tokens.dtype
     dma = pltpu.SemaphoreType.DMA
@@ -448,7 +448,7 @@
             dma((3 + head_count,)),
         ],
         compiler_params=pltpu.CompilerParams(
-            collective_id=0, has_side_effects=True, vmem_limit_bytes=60 * 2**20
+            collective_id=0, has_side_effects=True, vmem_limit_bytes=int(53.6 * 2**20)
         ),
     )(
         query_tokens,

time: 60.4 us -> 56.6 us (0.937)
  the two profiles are of different devices: /device:TPU:25 before, /device:TPU:1 now
where the time goes in v3:
time: 56.6 us; the launch traced here: 56.5 us
  Pallas kernels  53.3 us (94%)
  other arithmetic  1.64 us (3%)
  local copies, waits for them, and re-layouts  1.47 us (3%)
    pallas_call x1, Pallas kernels, per_device(): pl.pallas_call(functools.partial(kernel, n, heads), out_shape=jax.ShapeDt...  53.3 us

profile of v3, /device:TPU:1, one launch (start us, length us, event | category | flops | bytes accessed | tf_op | source)
XLA Modules:
  0.0 56.5 jit_solution(7024392286226371412)
XLA Ops:
  0.0 0.7 %iota_compare_fusion = pred[2,12]{1,0:T(4,128)(4,1)S(1)} fusion(s32[2]{0:T(128)} %param.15), kind=kLoop, calls=%fused_computation.27 | loop fusion | flops 24 | bytes 32 | tf_op jit(solution)/shard_map/lt | solution.py:393
  0.8 0.7 %and_select_fusion.10 = (s32[2,12]{1,0:T(2,128)S(1)}, s32[2,12]{1,0:T(2,128)S(1)}) fusion(s32[2,12]{1,0:T(2,128)} %param.14), kind=kLoop, calls=%fused_computation.23 | loop fusion | flops 456 | bytes 288 | tf_op jit(solution)/shard_map/jit(floor_divide)/jit(_where)/select_n | solution.py:392
  1.4 0.1 fusion
  1.5 0.6 %slice.3.own_ref = s32[1]{0:T(128)} slice(s32[16]{0:T(128)S(1)} %fusion), slice={[8:9]} | slice | bytes 8 | tf_op jit(solution)/shard_map/slice | solution.py:460
  2.1 0.1 fusion.1
  2.2 0.1 broadcast_in_dim.37.ask_ref
  2.3 0.1 broadcast_in_dim.40
  2.4 53.3 %shard_map.82 = bf16[256,512]{1,0:T(8,128)(2,1)S(1)} custom-call(bf16[256,1024]{1,0:T(8,128)(2,1)} %qt_hbm.1, bf16[8,2,64,1024]{3,2,1,0:T(8,128)(2,1)} %bitcast.5, bf16[1024,512]{1,0:T(8,128)(2,1)} %wq_hbm.1, bf16[1024,512]{1,0:T(8,128)(2,1)} %wk_hbm.1, bf16[1024,512]{1,0:T(8,128)(2,1)} %wv_hbm.1, bf16[512,1024]{1,0:T(8,128)(2,1)} %wo_hbm.1, ...), custom_call_target="tpu_custom_call" | custom-call | tf_op jit(solution)/shard_map/pallas_call | solution.py:407
  55.8 0.7 %copy.16 = bf16[256,512]{1,0:T(8,128)(2,1)} copy(bf16[256,512]{1,0:T(8,128)(2,1)S(1)} %shard_map.82) | data formatting | bytes 524288
  (4 shorter events, 0.1 us)
